TPU v7x, 128 devices: a whole 4x4x4 slice. The times are simulated.
128 devices in a mesh: lat: 4 (over x_hi, core), lon: 32 (over y, x_lo, z).
Axes of the slice: x: 4 (x_hi: 2, x_lo: 2; x = x_hi * 2 + x_lo), y: 4, z: 4, core: 2. Of those that a mesh axis runs over, the one named last changes fastest.
Arguments:
- inputs: bfloat16 [32, 10240, 512], P('lat', 'lon'), may hold values from -6 to 6
- w_conv: bfloat16 [512, 512], replicated, may hold values from -0.25 to 0.25
- w_point: bfloat16 [512, 512], replicated, may hold values from -0.25 to 0.25
- cotangent: bfloat16 [32, 2560, 512], P('lat', 'lon'), may hold values from -6 to 6
Outputs:
- encoded: bfloat16 [32, 2560, 512], P('lat', 'lon')
- grad_inputs: bfloat16 [32, 10240, 512], P('lat', 'lon')
- grad_conv: float32 [512, 512], P(None, ('lat', 'lon'))
- grad_point: float32 [512, 512], P(None, ('lat', 'lon'))
All inputs are finite; a program needn't handle non-finite values.
Results may differ from a plain program's by a relative error of at most 0.005.
Values may be sent and summed in bfloat16 or wider, within the bound.
A program may use at most 128 MiB of HBM per device.

v0:
```python
import math

import jax
import jax.numpy as jnp
from jax import lax
from jax.sharding import PartitionSpec as P

G = 8
KW = 8


def padded_2(array, sides, width):
    for axis, dim in sides:
        size, length = (lax.axis_size(axis), array.shape[dim])
        up = [(i, (i + 1) % size) for i in range(size)]
        down = [(j, i) for i, j in up]
        last = lax.slice_in_dim(array, length - width, length, axis=dim)
        first = lax.slice_in_dim(array, 0, width, axis=dim)
        before = lax.ppermute(last, axis, up)
        after = lax.ppermute(first, axis, down)
        array = jnp.concatenate([before, array, after], axis=dim)
    return array


def from_behind(block, axis, distance):
    devices = range(lax.axis_size(axis))
    route = [((i - distance) % len(devices), i) for i in devices]
    return lax.ppermute(block, axis, route)


def build_patches(padded, out_cols):
    band_rows = padded.shape[0]
    channels = padded.shape[2]
    front = padded[:, : 4 * out_cols].reshape(band_rows, out_cols, 4, channels)
    behind = padded[:, 4 : 4 * out_cols + 4].reshape(band_rows, out_cols, 4, channels)
    return jnp.concatenate([front, behind], 2)


def spread_back(pre_split, kernel, out_cols):
    band_rows = pre_split.shape[0]
    channels = pre_split.shape[2] * pre_split.shape[3]
    patch_grad = jnp.einsum(
        "rpgo,kigo->rpkgi", pre_split, kernel, preferred_element_type=jnp.float32
    )
    front = patch_grad[:, :, :4].reshape(band_rows, 4 * out_cols, channels)
    behind = patch_grad[:, :, 4:].reshape(band_rows, 4 * out_cols, channels)
    zeros_four = jnp.zeros((band_rows, 4, channels), jnp.float32)
    return jnp.concatenate([front, zeros_four], 1) + jnp.concatenate([zeros_four, behind], 1)


def per_device(inputs, w_conv, w_point, cotangent):
    band_rows, columns, channels = inputs.shape
    out_cols = columns // 4
    group_size = channels // G
    padded = padded_2(inputs, (("lon", 1),), 2)
    patches = build_patches(padded, out_cols).reshape(band_rows, out_cols, KW, G, group_size)
    kernel = w_conv.reshape(KW, group_size, G, group_size)
    preact = jnp.einsum(
        "rpkgi,kigo->rpgo", patches, kernel, preferred_element_type=jnp.float32
    ).reshape(band_rows * out_cols, channels)
    activated, gelu_back = jax.vjp(jax.nn.gelu, preact)
    act_bf = activated.astype(jnp.bfloat16)
    encoded = (
        jnp.dot(act_bf, w_point, preferred_element_type=jnp.float32)
        .astype(jnp.bfloat16)
        .reshape(band_rows, out_cols, channels)
    )
    flat_cot = cotangent.reshape(band_rows * out_cols, channels)
    point_term = lax.dot_general(
        act_bf, flat_cot, (((0,), (0,)), ((), ())), preferred_element_type=jnp.float32
    )
    act_grad = lax.dot_general(
        flat_cot, w_point, (((1,), (1,)), ((), ())), preferred_element_type=jnp.float32
    )
    pre_grad = gelu_back(act_grad)[0].astype(jnp.bfloat16)
    pre_split = pre_grad.reshape(band_rows, out_cols, G, group_size)
    conv_term = jnp.einsum(
        "rpkgi,rpgo->kigo", patches, pre_split, preferred_element_type=jnp.float32
    ).reshape(KW * group_size, channels)
    extended = spread_back(pre_split, kernel, out_cols)
    middle = extended[:, 2 : columns + 2]
    from_west = from_behind(extended[:, columns + 2 :].astype(jnp.bfloat16), "lon", 1).astype(
        jnp.float32
    )
    from_east = from_behind(extended[:, :2].astype(jnp.bfloat16), "lon", -1).astype(jnp.float32)
    owned = jnp.concatenate(
        [
            middle[:, :2] + from_west,
            middle[:, 2 : columns - 2],
            middle[:, columns - 2 :] + from_east,
        ],
        1,
    )
    grad_inputs = owned.astype(jnp.bfloat16)
    grad_scale = 1.0 / math.sqrt(band_rows * lax.axis_size("lat") * out_cols * lax.axis_size("lon"))
    conv_sum, point_sum = (
        lax.psum_scatter(conv_term, ("lat", "lon"), scatter_dimension=1, tiled=True),
        lax.psum_scatter(point_term, ("lat", "lon"), scatter_dimension=1, tiled=True),
    )
    return (encoded, grad_inputs, conv_sum * grad_scale, point_sum * grad_scale)


def solution(mesh):
    placed = (P("lat", "lon", None), P(), P(), P("lat", "lon", None))
    return jax.shard_map(
        per_device,
        mesh=mesh,
        in_specs=placed,
        out_specs=(
            P("lat", "lon", None),
            P("lat", "lon", None),
            P(None, ("lat", "lon")),
            P(None, ("lat", "lon")),
        ),
        check_vma=False,
    )
```

profile of v0, /device:TPU:0, one launch (start us, length us, event | category | flops | bytes accessed | tf_op | source)
XLA Modules:
  0.0 304.5 jit_solution(4504805940046627326)
XLA Ops:
  7.2 1.0 fusion.40
  8.2 2.1 collective-permute-start
  10.3 5.6 %collective-permute-start.1 = (bf16[8,2,512]{2,1,0:T(2,128)(2,1)S(1)}, bf16[8,2,512]{2,1,0:T(2,128)(2,1)S(1)}, u32[]{:S(2)}, u32[]{:S(2)}) collective-permute-start(bf16[8,2,512]{2,1,0:T(2,128)(2,1)S(1)} %get-tuple-element.15), channel_id=1, source_target_pairs={{1,0},{2,1},{3,2},{4,3},{5,4},{6,5},{7,6},{8,7},{9,8},{10,9},{11,1... | collective-permute-start | bytes 49160 | tf_op jit(solution)/shard_map/ppermute | solution.py:20
  15.9 2.4 reshape.40
  18.2 5.0 %pad_maximum_fusion.2 = (bf16[8,320,512]{2,1,0:T(8,128)(2,1)}, bf16[8,320,512]{2,1,0:T(8,128)(2,1)S(1)}) fusion(bf16[8,320,512]{2,1,0:T(8,128)(2,1)} %param.4, bf16[8,2,512]{2,1,0:T(2,128)(2,1)S(1)} %collective-permute-done, bf16[8,2,512]{2,1,0:T(2,128)(2,1)S(1)} %collective-permute-done.1), kind=kLoop, calls=%fused_computation.11 | loop fusion | flops 10485760 | bytes 7897088 | tf_op jit(solution)/shard_map/concatenate | solution.py:21
  23.3 7.5 %concatenate.26 = bf16[8,80,4,8,64]{4,3,2,1,0:T(8,128)(2,1)} reshape(bf16[8,320,512]{2,1,0:T(8,128)(2,1)} %get-tuple-element.12) | data formatting | bytes 5242880 | tf_op jit(solution)/shard_map/concatenate | solution.py:36
  30.7 9.1 %copy.33 = bf16[8,80,4,8,64]{1,4,2,0,3:T(8,128)(2,1)} copy(bf16[8,80,4,8,64]{4,3,2,1,0:T(8,128)(2,1)} %concatenate.26) | data formatting | bytes 5242880 | tf_op jit(solution)/shard_map/concatenate | solution.py:36
  39.8 4.6 %concatenate.28 = bf16[8,80,4,8,64]{4,3,2,1,0:T(8,128)(2,1)} reshape(bf16[8,320,512]{2,1,0:T(8,128)(2,1)S(1)} %get-tuple-element.13) | data formatting | bytes 5242880 | tf_op jit(solution)/shard_map/concatenate | solution.py:36
  44.4 9.2 %copy.34 = bf16[8,80,4,8,64]{1,4,2,0,3:T(8,128)(2,1)} copy(bf16[8,80,4,8,64]{4,3,2,1,0:T(8,128)(2,1)} %concatenate.28) | data formatting | bytes 5242880 | tf_op jit(solution)/shard_map/concatenate | solution.py:36
  53.6 7.0 %fusion.9 = (bf16[8,80,8,64]{1,3,0,2:T(8,128)(2,1)}, f32[8,80,8,64]{1,3,0,2:T(8,128)}) fusion(bf16[8,80,4,8,64]{1,4,2,0,3:T(8,128)(2,1)} %copy.34, bf16[8,80,4,8,64]{1,4,2,0,3:T(8,128)(2,1)} %copy.33, bf16[8,64,8,64,1]{3,2,1,0,4:T(8,128)(2,1)S(1)} %bitcast.43), kind=kOutput, calls=%fused_computation.20 | convolution fusion | flops 348979200 | bytes 7733248 | tf_op jit(solution)/shard_map/rpkgi,kigo->rpgo/dot_general | solution.py:58
  60.6 2.2 copy.68
  62.8 1.7 reshape.55
  64.5 2.7 fusion.19
  67.5 1.0 reshape.44
  68.5 7.6 %fusion.10 = f32[8,64,8,64]{1,3,0,2:T(8,128)} fusion(bf16[8,80,8,64,1]{1,0,3,2,4:T(8,128)(2,1)S(1)} %bitcast.45, bf16[8,80,4,8,64]{1,4,2,0,3:T(8,128)(2,1)} %copy.34, bf16[8,80,4,8,64]{1,4,2,0,3:T(8,128)(2,1)} %copy.33), kind=kOutput, calls=%fused_computation.23 | convolution fusion | flops 338165760 | bytes 6946816 | tf_op jit(solution)/shard_map/rpkgi,rpgo->kigo/dot_general | solution.py:77
  76.1 8.0 %convolution_bitcast_fusion = f32[8,80,8,8,64]{1,4,2,0,3:T(8,128)} fusion(bf16[8,80,8,64,1]{1,0,3,2,4:T(8,128)(2,1)S(1)} %bitcast.46, bf16[8,64,8,64,1]{3,2,1,0,4:T(8,128)(2,1)S(1)} %bitcast.44), kind=kOutput, calls=%fused_computation | convolution fusion | flops 335544320 | bytes 11665408 | tf_op jit(solution)/shard_map/rpgo,kigo->rpkgi/dot_general | solution.py:42
  84.8 0.8 convert_element_type.29
  85.7 1.6 fusion.41
  87.3 1.2 copy.67
  88.5 1.5 reshape.54
  89.9 10.9 %fusion.38 = (f32[8,80,4,8,64]{1,4,2,0,3:T(8,128)}, f32[8,80,4,8,64]{1,4,2,0,3:T(8,128)}) fusion(f32[8,80,8,8,64]{1,4,2,0,3:T(8,128)} %convolution_bitcast_fusion), kind=kLoop, calls=%fused_computation.54 | loop fusion | bytes 20971520 | tf_op jit(solution)/shard_map/slice | solution.py:45
  100.8 12.5 %copy.46 = f32[8,80,4,8,64]{4,3,2,1,0:T(8,128)} copy(f32[8,80,4,8,64]{1,4,2,0,3:T(8,128)} %get-tuple-element.6) | data formatting | bytes 10485760 | tf_op jit(solution)/shard_map/slice | solution.py:45
  113.3 9.5 %reshape.45 = f32[8,320,512]{2,1,0:T(8,128)} reshape(f32[8,80,4,8,64]{4,3,2,1,0:T(8,128)} %copy.46) | data formatting | bytes 10485760 | tf_op jit(solution)/shard_map/reshape | solution.py:45
  122.8 12.5 %copy.47 = f32[8,80,4,8,64]{4,3,2,1,0:T(8,128)} copy(f32[8,80,4,8,64]{1,4,2,0,3:T(8,128)} %get-tuple-element.7) | data formatting | bytes 10485760 | tf_op jit(solution)/shard_map/slice | solution.py:46
  135.3 9.4 %reshape.46 = f32[8,320,512]{2,1,0:T(8,128)} reshape(f32[8,80,4,8,64]{4,3,2,1,0:T(8,128)} %copy.47) | data formatting | bytes 10485760 | tf_op jit(solution)/shard_map/reshape | solution.py:46
  144.7 5.6 %add_convert_fusion = bf16[8,324,512]{2,1,0:T(8,128)(2,1)S(1)} fusion(f32[8,320,512]{2,1,0:T(8,128)} %reshape.46, f32[8,320,512]{2,1,0:T(8,128)} %reshape.45), kind=kLoop, calls=%fused_computation.4 | loop fusion | flops 2654208 | bytes 13139968 | tf_op jit(solution)/shard_map/convert.5
  150.5 6.2 %collective-permute-start.3 = (bf16[8,2,512]{2,1,0:T(2,128)(2,1)S(1)}, bf16[8,2,512]{2,1,0:T(2,128)(2,1)S(1)}, u32[]{:S(2)}, u32[]{:S(2)}) collective-permute-start(bf16[8,2,512]{2,1,0:T(2,128)(2,1)S(1)} %get-tuple-element.11), channel_id=1, source_target_pairs={{1,0},{2,1},{3,2},{4,3},{5,4},{6,5},{7,6},{8,7},{9,8},{10,9},{11,1... | collective-permute-start | bytes 49160 | tf_op jit(solution)/shard_map/ppermute | solution.py:28
  156.7 1.4 convolution_convert_fusion
  158.9 1.8 copy-done.2
  160.8 2.2 pad_maximum_fusion.3
  163.0 133.4 %all-reduce.7.cloned.1.call-done = (f32[512,512]{0,1:T(8,128)}, f32[512,512]{0,1:T(8,128)}) async-done(((f32[512,512]{0,1:T(8,128)}, f32[512,512]{0,1:T(8,128)}), (f32[512,512]{0,1:T(8,128)}, f32[512,512]{0,1:T(8,128)})) %all-reduce.7.cloned.1.call-update) | async-done | bytes 2097168
  296.3 1.3 dynamic-slice_multiply_fusion
  (34 shorter events, 2.0 us)
Async XLA Ops:
  7.2 57.3 %copy-start = (bf16[8,80,512]{2,1,0:T(8,128)(2,1)S(1)}, bf16[8,80,512]{2,1,0:T(8,128)(2,1)}, u32[]{:S(2)}) copy-start(bf16[8,80,512]{2,1,0:T(8,128)(2,1)} %param.7) | copy-start | bytes 1966084
  7.2 289.2 %all-reduce.7.cloned.1.call-start = ((), (), s32[]{:S(2)}) async-start(), calls=%async_computation | async-start | bytes 4194304
  8.2 10.1 %collective-permute-start = (bf16[8,2,512]{2,1,0:T(2,128)(2,1)S(1)}, bf16[8,2,512]{2,1,0:T(2,128)(2,1)S(1)}, u32[]{:S(2)}, u32[]{:S(2)}) collective-permute-start(bf16[8,2,512]{2,1,0:T(2,128)(2,1)S(1)} %get-tuple-element.14), channel_id=1, source_target_pairs={{0,1},{1,2},{2,3},{3,4},{4,5},{5,6},{6,7},{7,8},{8,9},{9,10},{10,1... | collective-permute-start | bytes 49160 | tf_op jit(solution)/shard_map/ppermute | solution.py:19
  10.3 8.0 %collective-permute-start.1 = (bf16[8,2,512]{2,1,0:T(2,128)(2,1)S(1)}, bf16[8,2,512]{2,1,0:T(2,128)(2,1)S(1)}, u32[]{:S(2)}, u32[]{:S(2)}) collective-permute-start(bf16[8,2,512]{2,1,0:T(2,128)(2,1)S(1)} %get-tuple-element.15), channel_id=1, source_target_pairs={{1,0},{2,1},{3,2},{4,3},{5,4},{6,5},{7,6},{8,7},{9,8},{10,9},{11,1... | collective-permute-start | bytes 49160 | tf_op jit(solution)/shard_map/ppermute | solution.py:20
  44.4 9.2 %copy-start.3 = (bf16[8,64,8,64]{3,2,1,0:T(8,128)(2,1)S(1)}, bf16[8,64,8,64]{3,2,1,0:T(8,128)(2,1)}, u32[]{:S(2)}) copy-start(bf16[8,64,8,64]{3,2,1,0:T(8,128)(2,1)} %reshape.40) | copy-start | bytes 1572868
  68.5 7.6 %copy-start.4 = (bf16[8,64,8,64]{3,2,1,0:T(8,128)(2,1)S(1)}, bf16[8,64,8,64]{3,2,1,0:T(8,128)(2,1)}, u32[]{:S(2)}) copy-start(bf16[8,64,8,64]{3,2,1,0:T(8,128)(2,1)} %reshape.40) | copy-start | bytes 1572868
  76.1 8.0 %copy-start.7 = (bf16[8,80,8,64]{1,3,0,2:T(8,128)(2,1)S(1)}, bf16[8,80,8,64]{1,3,0,2:T(8,128)(2,1)}, u32[]{:S(2)}) copy-start(bf16[8,80,8,64]{1,3,0,2:T(8,128)(2,1)} %get-tuple-element.16) | copy-start | bytes 1966084
  85.6 1.6 copy-start.5
  144.7 14.2 %slice-start = ((s8[5242880]{0:T(1024)(128)(4,1)}), s8[1048576]{0:T(1024)(128)(4,1)S(1)}, s32[]{:S(2)}) async-start(s8[5242880]{0:T(1024)(128)(4,1)} %bitcast.41), calls=%async_computation.1 | async-start | bytes 2097152
  144.7 12.0 %copy-start.6 = (f32[640,512]{1,0:T(8,128)S(1)}, f32[640,512]{1,0:T(8,128)}, u32[]{:S(2)}) copy-start(f32[640,512]{1,0:T(8,128)} %reshape.55) | copy-start | bytes 3932164
  144.7 12.0 %copy-start.8 = (bf16[512,512]{1,0:T(8,128)(2,1)S(1)}, bf16[512,512]{1,0:T(8,128)(2,1)}, u32[]{:S(2)}) copy-start(bf16[512,512]{1,0:T(8,128)(2,1)} %param.6) | copy-start | bytes 1572868
  144.7 14.2 %slice-start.1 = ((s8[5242880]{0:T(1024)(128)(4,1)}), s8[4194304]{0:T(1024)(128)(4,1)S(1)}, s32[]{:S(2)}) async-start(s8[5242880]{0:T(1024)(128)(4,1)} %bitcast.41), calls=%async_computation.2 | async-start | bytes 8388608
  150.4 8.4 %collective-permute-start.2 = (bf16[8,2,512]{2,1,0:T(2,128)(2,1)S(1)}, bf16[8,2,512]{2,1,0:T(2,128)(2,1)S(1)}, u32[]{:S(2)}, u32[]{:S(2)}) collective-permute-start(bf16[8,2,512]{2,1,0:T(2,128)(2,1)S(1)} %get-tuple-element.10), channel_id=1, source_target_pairs={{31,0},{0,1},{1,2},{2,3},{3,4},{4,5},{5,6},{6,7},{7,8},{8,9},{9,10... | collective-permute-start | bytes 49160 | tf_op jit(solution)/shard_map/ppermute | solution.py:28
  150.5 8.4 %collective-permute-start.3 = (bf16[8,2,512]{2,1,0:T(2,128)(2,1)S(1)}, bf16[8,2,512]{2,1,0:T(2,128)(2,1)S(1)}, u32[]{:S(2)}, u32[]{:S(2)}) collective-permute-start(bf16[8,2,512]{2,1,0:T(2,128)(2,1)S(1)} %get-tuple-element.11), channel_id=1, source_target_pairs={{1,0},{2,1},{3,2},{4,3},{5,4},{6,5},{7,6},{8,7},{9,8},{10,9},{11,1... | collective-permute-start | bytes 49160 | tf_op jit(solution)/shard_map/ppermute | solution.py:28
  158.2 2.5 copy-start.2
  160.8 136.9 %copy-start.1 = (bf16[8,80,512]{2,1,0:T(8,128)(2,1)S(1)}, bf16[8,80,512]{2,1,0:T(8,128)(2,1)}, u32[]{:S(2)}) copy-start(bf16[8,80,512]{2,1,0:T(8,128)(2,1)} %param.7) | copy-start | bytes 1966084
Sparse Core Ops, SparseCore 0:
  144.8 151.4 all-reduce.6
where the time goes:
time: 307 us; the launch traced here: 305 us
  waiting for transfers between devices  133 us (43%)
  local copies, waits for them, and re-layouts  100 us (33%)
  matrix products  28.3 us (9%)
  other arithmetic  14.3 us (5%)
  between operations  14.2 us (5%)
  starting transfers between devices  14 us (5%)
    unnamed x2, waiting for transfers between devices  133 us
    concatenate x4, local copies, waits for them, and re-layouts, build_patches(): return jnp.concatenate([front, behind], 2)  30.3 us
    slice x2, local copies, waits for them, and re-layouts, spread_back(): front = patch_grad[:, :, :4].reshape(band_rows, 4 * out_cols, channels)  23.4 us
    slice x1, local copies, waits for them, and re-layouts, spread_back(): behind = patch_grad[:, :, 4:].reshape(band_rows, 4 * out_cols, channels)  12.5 us
    reshape x1, local copies, waits for them, and re-layouts, spread_back(): front = patch_grad[:, :, :4].reshape(band_rows, 4 * out_cols, channels)  9.47 us
    reshape x1, local copies, waits for them, and re-layouts, spread_back(): behind = patch_grad[:, :, 4:].reshape(band_rows, 4 * out_cols, channels)  9.41 us
    dot_general x1, matrix products, spread_back(): jnp.einsum('rpgo,kigo->rpkgi', pre_split, kernel, preferred_element_type=...  8.03 us
    dot_general x1, matrix products, per_device(): jnp.einsum('rpkgi,rpgo->kigo', patches, pre_split, preferred_element_type...  7.55 us
  transfers between devices with their start and end apart: 5, of which 1 were waited for; matrix products, arithmetic and copies ran while one was open for 4% of the time, Pallas kernels for 0%

commit v1 on v0

v1 whole, which is shorter than its diff:
```python
import functools
import math

import jax
import jax.numpy as jnp
from jax import lax
from jax.experimental import pallas as pl
from jax.experimental.pallas import tpu as pltpu
from jax.sharding import PartitionSpec as P

MESH = pl.DeviceIdType.MESH
F32 = jnp.float32
BF16 = jnp.bfloat16
G = 8
KW = 8
C = 512
HALF = 256
GELU_C = math.sqrt(2.0 / math.pi)
GELU_A = 0.044715


def nt_dot(a, b):
    return lax.dot_general(a, b, (((1,), (1,)), ((), ())), preferred_element_type=F32)


def dot(a, b):
    return jnp.dot(a, b, preferred_element_type=F32)


def messages(rows8):
    low = lax.broadcasted_iota(jnp.int32, (8, 128), 0) < 4
    tiles = [rows8[:, l * 128 : (l + 1) * 128] for l in range(4)]
    rolled = [pltpu.roll(t, 4, 0) for t in tiles]
    even = [jnp.where(low, tiles[a], rolled[a + 1]) for a in (0, 2)]
    odd = [jnp.where(low, rolled[a], tiles[a + 1]) for a in (0, 2)]
    return jnp.concatenate(even, 0), jnp.concatenate(odd, 0)


def body(
    n_lat, n_lon, scale, x_hbm, wc_hbm, wp_hbm, cot_hbm,
    enc_hbm, gin_hbm, gconv_ref, gpoint_ref,
    xb, x32, wc, wp, cot, halo_w, halo_e, chalo_w, chalo_e, c32,
    wd, pt, pe, preact, agrad, act, pre, pre_t, cot_t, pre32, pm, pp, enc, gout,
    sums, csend, crecv, msend, mrecv,
    x_sem, in_sem, out_sem, gout_sem, halo_send, halo_recv, c_sem_s, c_sem_r, m_sem_s, m_sem_r,
):
    lat, cols = x_hbm.shape[0], x_hbm.shape[1]
    out_cols = cols // 4
    main = lat * out_cols
    span = cols + 16
    pspan = out_cols + 16
    my_lat = lax.axis_index("lat")
    my_lon = lax.axis_index("lon")
    core = lax.rem(my_lat, 2)
    my_xhi = my_lat // 2
    chips = (n_lat // 2) * n_lon
    my_chip = my_xhi * n_lon + my_lon

    def peer(i):
        chip = lax.rem(my_chip + i, chips)
        return (chip // n_lon * 2 + core, lax.rem(chip, n_lon))

    partner = (my_xhi * 2 + 1 - core, my_lon)
    west = (my_lat, lax.rem(my_lon + n_lon - 1, n_lon))
    east = (my_lat, lax.rem(my_lon + 1, n_lon))

    barrier = pltpu.get_barrier_semaphore()

    def say(i, carry):
        pl.semaphore_signal(barrier, inc=1, device_id=peer(i), device_id_type=MESH)
        return carry

    lax.fori_loop(1, chips, say, 0)
    pl.semaphore_signal(barrier, inc=1, device_id=partner, device_id_type=MESH)

    wc_copy = pltpu.make_async_copy(wc_hbm, wc, in_sem.at[0])
    wp_copy = pltpu.make_async_copy(wp_hbm, wp, in_sem.at[1])
    cot_copy = pltpu.make_async_copy(cot_hbm, cot, in_sem.at[2])

    def x_copy(r):
        return pltpu.make_async_copy(x_hbm.at[r], xb.at[r], x_sem.at[r])

    wc_copy.start()
    for r in range(lat):
        x_copy(r).start()
    cot_copy.start()
    wp_copy.start()

    wc_copy.wait()
    lane_group = lax.broadcasted_iota(jnp.int32, (64, HALF), 1) // 64

    def spread(k, carry):
        for h in range(2):
            block = wc[pl.ds(pl.multiple_of(k * 64, 64), 64), h * HALF : (h + 1) * HALF].astype(F32)
            for g in range(4):
                at = pl.ds(pl.multiple_of(k * HALF + g * 64, 64), 64)
                wd[h, at, :] = jnp.where(lane_group == g, block, 0.0).astype(BF16)
        return carry

    lax.fori_loop(0, KW, spread, 0)

    def tap_lanes(k, l):
        start = k * HALF + (l % 2) * 128
        return slice(start, start + 128)

    def widen(r, carry):
        x_copy(r).wait()
        base = r * span
        zero = jnp.zeros((8, 128), F32)
        at = pl.ds(pl.multiple_of(r * out_cols, 16), out_cols)
        for l in range(4):
            x32[l, pl.ds(pl.multiple_of(base, 8), 8), :] = zero
            x32[l, pl.ds(pl.multiple_of(base + 8 + cols, 8), 8), :] = zero
            for s in range(0, cols, 16):
                x32[l, pl.ds(pl.multiple_of(base + 8 + s, 8), 16), :] = xb[
                    r, s : s + 16, l * 128 : (l + 1) * 128
                ].astype(F32)
        for k in range(KW):
            for l in range(4):
                taken = x32[l, pl.ds(base + 6 + k, out_cols, stride=4), :].astype(BF16)
                pt[l // 2, at, tap_lanes(k, l)] = taken
        return carry

    lax.fori_loop(0, lat, widen, 0)

    pl.semaphore_wait(barrier, chips)

    def remote(src, dst, to, s, r):
        return pltpu.make_async_remote_copy(
            src_ref=src, dst_ref=dst, send_sem=s, recv_sem=r, device_id=to, device_id_type=MESH
        )

    halos = [
        remote(x_hbm.at[:, 0:8, :], halo_e, west, halo_send.at[0], halo_recv.at[0]),
        remote(x_hbm.at[:, cols - 8 : cols, :], halo_w, east, halo_send.at[1], halo_recv.at[1]),
        remote(cot_hbm.at[:, 0:8, :], chalo_e, west, halo_send.at[2], halo_recv.at[2]),
        remote(cot_hbm.at[:, out_cols - 8 : out_cols, :], chalo_w, east, halo_send.at[3], halo_recv.at[3]),
    ]
    for h in halos:
        h.start()

    cot_copy.wait()
    wp_copy.wait()
    cot2 = cot[...].reshape(main, C)
    cot_t[...] = cot2.T
    agrad[0:main, :] = nt_dot(cot2, wp[...])

    step = main // 2

    def forward(c, carry):
        at = pl.ds(pl.multiple_of(c * step, 16), step)
        for h in range(2):
            y = dot(pt[h, at, :], wd[h])
            for i in range(2):
                preact[2 * h + i, at, :] = y[:, i * 128 : (i + 1) * 128]
        return carry

    lax.fori_loop(0, 2, forward, 0)

    for h in halos:
        h.wait()
    for r in range(lat):
        for l in range(4):
            lanes = slice(l * 128, (l + 1) * 128)
            x32[l, r * span : r * span + 8, :] = halo_w[r, :, lanes].astype(F32)
            x32[l, r * span + 8 + cols : r * span + 16 + cols, :] = halo_e[r, :, lanes].astype(F32)
            c32[l, r * 8 : r * 8 + 8, :] = chalo_w[r, :, lanes].astype(F32)
            c32[l, (lat + r) * 8 : (lat + r) * 8 + 8, :] = chalo_e[r, :, lanes].astype(F32)
    for r in range(lat):
        for k, j in ((0, 0), (1, 0), (6, out_cols - 16), (7, out_cols - 16)):
            for l in range(4):
                taken = x32[l, pl.ds(r * span + 6 + k + 4 * j, 16, stride=4), :].astype(BF16)
                pt[l // 2, r * out_cols + j : r * out_cols + j + 16, tap_lanes(k, l)] = taken
    for k in range(KW):
        for l in range(4):
            rows = [
                x32[l, pl.ds(4 * j + 6 + k, lat, stride=span), :]
                for j in (-1, out_cols, 0, out_cols - 1)
            ]
            pe[l // 2, :, tap_lanes(k, l)] = jnp.concatenate(rows, 0).astype(BF16)
    for h in range(2):
        edge = dot(pe[h], wd[h])
        for i in range(2):
            part = edge[:, i * 128 : (i + 1) * 128]
            preact[2 * h + i, main : main + 16, :] = part[0:16]
            preact[2 * h + i, pl.ds(0, lat, stride=out_cols), :] = part[16:24]
            preact[2 * h + i, pl.ds(out_cols - 1, lat, stride=out_cols), :] = part[24:32]
    cot_edge = jnp.concatenate(
        [
            jnp.concatenate(
                [c32[l, pl.ds(7, lat, stride=8), :], c32[l, pl.ds(lat * 8, lat, stride=8), :]], 0
            )
            for l in range(4)
        ],
        1,
    ).astype(BF16)
    agrad[main : main + 16, :] = nt_dot(cot_edge, wp[...])

    def gelu(at, l):
        z = preact[l, at, :]
        z2 = z * z
        th = jnp.tanh(GELU_C * (z + GELU_A * (z2 * z)))
        cdf = 0.5 * (1.0 + th)
        slope = cdf + (0.5 * z) * (1.0 - th * th) * (GELU_C * (1.0 + 3.0 * GELU_A * z2))
        return z * cdf, (agrad[at, l * 128 : (l + 1) * 128] * slope).astype(BF16)

    tiles = out_cols // 16

    def activate(r, carry):
        for t in range(tiles):
            at = pl.ds(pl.multiple_of(r * out_cols + t * 16, 16), 16)
            for l in range(4):
                lanes = slice(l * 128, (l + 1) * 128)
                a, p = gelu(at, l)
                act[at, lanes] = a.astype(BF16)
                pre[at, lanes] = p
                pre32[l, pl.ds(pl.multiple_of(r * pspan + 8 + t * 16, 8), 16), :] = p.astype(F32)
        return carry

    lax.fori_loop(0, lat, activate, 0)
    for l in range(4):
        edge_pre = gelu(slice(main, main + 16), l)[1].astype(F32)
        pre32[l, pl.ds(7, lat, stride=pspan), :] = edge_pre[0:8]
        pre32[l, pl.ds(8 + out_cols, lat, stride=pspan), :] = edge_pre[8:16]

    def core_rows(q, i):
        return pl.ds(pl.multiple_of((i // 16) * HALF + q * 128 + lax.rem(i, 16) * 8, 8), 8)

    def send_half(which):
        def one(i, carry):
            even, odd = messages(sums[which, core_rows(1 - core, i), :])
            csend[which, 2 * i] = even.astype(BF16)
            csend[which, 2 * i + 1] = odd.astype(BF16)
            return carry

        lax.fori_loop(0, 32, one, 0)
        pair(which).start()

    def pair(which):
        return remote(csend.at[which], crecv.at[which], partner, c_sem_s.at[which], c_sem_r.at[which])

    def send_all(which):
        pair(which).wait()

        def one(i, carry):
            even, odd = messages(sums[which, core_rows(core, i), :])
            msend[which, 2 * i] = (even + crecv[which, 2 * i].astype(F32)).astype(BF16)
            msend[which, 2 * i + 1] = (odd + crecv[which, 2 * i + 1].astype(F32)).astype(BF16)
            return carry

        lax.fori_loop(0, 32, one, 0)

        def push(i, carry):
            chip = lax.rem(my_chip + i, chips)
            remote(
                msend.at[which, chip], mrecv.at[which, i - 1], peer(i), m_sem_s.at[which], m_sem_r.at[which]
            ).start()
            return carry

        lax.fori_loop(1, chips, push, 0)

    def collect(which, out_ref):
        everything = pltpu.make_async_copy(
            msend.at[which, 0 : chips - 1], mrecv.at[which], m_sem_r.at[which]
        )
        everything.wait()
        pltpu.make_async_copy(
            msend.at[which, 0 : chips - 1], mrecv.at[which], m_sem_s.at[which]
        ).wait()

        def one(i, carry):
            return carry + mrecv[which, i].astype(F32)

        total = lax.fori_loop(0, chips - 1, one, msend[which, my_chip].astype(F32), unroll=7)
        out_ref[...] = total * scale

    for c in range(2):
        rows = slice(c * HALF, (c + 1) * HALF)
        sums[0, rows, :] = dot(cot_t[rows, :], act[...])
    send_half(0)

    enc[...] = dot(act[...], wp[...]).astype(BF16).reshape(lat, out_cols, C)
    enc_copy = pltpu.make_async_copy(enc, enc_hbm, out_sem.at[0])
    enc_copy.start()
    pre_t[...] = pre[...].T
    send_all(0)

    low_lanes = lax.broadcasted_iota(jnp.int32, (64, 128), 1) < 64

    def conv_grad(p, carry):
        for h in range(2):
            lanes = pl.ds(pl.multiple_of(p * 2 * HALF, 2 * HALF), 2 * HALF)
            both = dot(pre_t[h * HALF : (h + 1) * HALF, :], pt[h, 0:main, lanes])
            for g in range(4):
                rows = slice(g * 64, g * 64 + 64)
                tile = (g // 2) * 128
                a = both[rows, tile : tile + 128]
                b = both[rows, HALF + tile : HALF + tile + 128]
                if g % 2 == 0:
                    b = pltpu.roll(b, 64, 1)
                else:
                    a = pltpu.roll(a, 64, 1)
                sums[1, h * HALF + g * 64 : h * HALF + g * 64 + 64, pl.ds(pl.multiple_of(p * 128, 128), 128)] = (
                    jnp.where(low_lanes, a, b)
                )
        return carry

    lax.fori_loop(0, KW // 2, conv_grad, 0)
    send_half(1)

    for r in range(lat):
        at = slice(r * out_cols, (r + 1) * out_cols)
        for l in range(4):
            lanes = slice(l * 128, (l + 1) * 128)
            pm[at, lanes] = pre32[l, r * pspan + 7 : r * pspan + 7 + out_cols, :].astype(BF16)
            pp[at, lanes] = pre32[l, r * pspan + 9 : r * pspan + 9 + out_cols, :].astype(BF16)
    send_all(1)

    gblock = 4

    def gout_copy(c):
        return pltpu.make_async_copy(
            gout.at[pl.ds(c * gblock, gblock)], gin_hbm.at[pl.ds(c * gblock, gblock)], gout_sem.at[c]
        )

    def input_grad(c, carry):
        rows = gblock * out_cols
        at = pl.ds(pl.multiple_of(c * rows, 16), rows)
        for h in range(2):
            lanes = slice(h * HALF, (h + 1) * HALF)
            here = pre[at, lanes]
            for m, (first, second, shifted) in enumerate(((2, 6, pm), (3, 7, pm), (4, 0, pp), (5, 1, pp))):
                y = nt_dot(here, wd[h, first * HALF : (first + 1) * HALF, :]) + nt_dot(
                    shifted[at, lanes], wd[h, second * HALF : (second + 1) * HALF, :]
                )
                for r in range(gblock):
                    for i in range(2):
                        x32[2 * h + i, pl.ds((c * gblock + r) * cols + m, out_cols, stride=4), :] = y[
                            r * out_cols : (r + 1) * out_cols, i * 128 : (i + 1) * 128
                        ]
        for r in range(gblock):
            row = c * gblock + r
            for s in range(0, cols, 16):
                for l in range(4):
                    gout[row, s : s + 16, l * 128 : (l + 1) * 128] = x32[
                        l, pl.ds(pl.multiple_of(row * cols + s, 16), 16), :
                    ].astype(BF16)
        gout_copy(c).start()
        return carry

    lax.fori_loop(0, lat // gblock, input_grad, 0)

    collect(0, gpoint_ref)
    collect(1, gconv_ref)
    enc_copy.wait()
    for c in range(lat // gblock):
        gout_copy(c).wait()


def per_device(n_lat, n_lon, inputs, w_conv, w_point, cotangent):
    lat, cols, channels = inputs.shape
    out_cols = cols // 4
    main = lat * out_cols
    chips = (n_lat // 2) * n_lon
    scale = 1.0 / math.sqrt(main * n_lat * n_lon)
    dma = pltpu.SemaphoreType.DMA
    scratch = [
        pltpu.VMEM((lat, cols, C), BF16),
        pltpu.VMEM((4, lat * (cols + 16), 128), F32),
        pltpu.VMEM((C, C), BF16),
        pltpu.VMEM((C, C), BF16),
        pltpu.VMEM((lat, out_cols, C), BF16),
        pltpu.VMEM((lat, 8, C), BF16),
        pltpu.VMEM((lat, 8, C), BF16),
        pltpu.VMEM((lat, 8, C), BF16),
        pltpu.VMEM((lat, 8, C), BF16),
        pltpu.VMEM((4, 2 * lat * 8, 128), F32),
        pltpu.VMEM((2, KW * HALF, HALF), BF16),
        pltpu.VMEM((2, main, KW * HALF), BF16),
        pltpu.VMEM((2, 32, KW * HALF), BF16),
        pltpu.VMEM((4, main + 16, 128), F32),
        pltpu.VMEM((main + 16, C), F32),
        pltpu.VMEM((main, C), BF16),
        pltpu.VMEM((main, C), BF16),
        pltpu.VMEM((C, main), BF16),
        pltpu.VMEM((C, main), BF16),
        pltpu.VMEM((4, lat * (out_cols + 16), 128), F32),
        pltpu.VMEM((main, C), BF16),
        pltpu.VMEM((main, C), BF16),
        pltpu.VMEM((lat, out_cols, C), BF16),
        pltpu.VMEM((lat, cols, C), BF16),
        pltpu.VMEM((2, C, C), F32),
        pltpu.VMEM((2, chips, 16, 128), BF16),
        pltpu.VMEM((2, chips, 16, 128), BF16),
        pltpu.VMEM((2, chips, 16, 128), BF16),
        pltpu.VMEM((2, chips - 1, 16, 128), BF16),
        dma((lat,)),
        dma((3,)),
        dma((1,)),
        dma((2,)),
        dma((4,)),
        dma((4,)),
        dma((2,)),
        dma((2,)),
        dma((2,)),
        dma((2,)),
    ]
    any_spec = pl.BlockSpec(memory_space=pl.ANY)
    vmem_spec = pl.BlockSpec(memory_space=pltpu.VMEM)
    encoded, grad_inputs, conv, point = pl.pallas_call(
        functools.partial(body, n_lat, n_lon, scale),
        out_shape=(
            jax.ShapeDtypeStruct((lat, out_cols, C), BF16),
            jax.ShapeDtypeStruct((lat, cols, C), BF16),
            jax.ShapeDtypeStruct((16, 128), F32),
            jax.ShapeDtypeStruct((16, 128), F32),
        ),
        in_specs=[any_spec] * 4,
        out_specs=(any_spec, any_spec, vmem_spec, vmem_spec),
        scratch_shapes=scratch,
        compiler_params=pltpu.CompilerParams(
            collective_id=0, has_side_effects=True, vmem_limit_bytes=60 * 1024 * 1024
        ),
        name="conv_step",
    )(inputs, w_conv, w_point, cotangent)

    def unfold(block):
        return block.reshape(4, 4, 128).transpose(0, 2, 1).reshape(C, 4)

    return encoded, grad_inputs, unfold(conv), unfold(point)


def solution(mesh):
    placed = (P("lat", "lon", None), P(), P(), P("lat", "lon", None))
    return jax.shard_map(
        functools.partial(per_device, mesh.shape["lat"], mesh.shape["lon"]),
        mesh=mesh,
        in_specs=placed,
        out_specs=(
            P("lat", "lon", None),
            P("lat", "lon", None),
            P(None, ("lat", "lon")),
            P(None, ("lat", "lon")),
        ),
        check_vma=False,
    )
```

time: 307 us -> 41.8 us (0.14)
  waiting for transfers between devices: 133 us -> 0 us
  local copies, waits for them, and re-layouts: 100 us -> 6.6 us
  Pallas kernels: 0 us -> 34.3 us
  matrix products: 28.3 us -> 0 us
  other arithmetic: 14.3 us -> 0 us
  starting transfers between devices: 14 us -> 0 us
  between operations: 14.2 us -> 0.64 us
    unnamed x2 -> x0, waiting for transfers between devices: 133 us -> none
    slice x6 -> x0, local copies, waits for them, and re-layouts: 37.6 us -> none  [the longest x2 23.4 us: spread_back(): front = patch_grad[:, :, :4].reshape(band_rows, 4 * out_cols, channels)]
    pallas_call x0 -> x1, Pallas kernels: none -> 34.3 us  [per_device(): pl.pallas_call(functools.partial(body, n_lat, n_lon, scale), out_shape=(j...]
    concatenate x4 -> x0, local copies, waits for them, and re-layouts: 30.3 us -> none  [build_patches(): return jnp.concatenate([front, behind], 2)]
    reshape x8 -> x0, local copies, waits for them, and re-layouts: 28.8 us -> none  [the longest x1 9.47 us: spread_back(): front = patch_grad[:, :, :4].reshape(band_rows, 4 * out_cols, channels)]
    dot_general x6 -> x0, matrix products: 28.3 us -> none  [the longest x1 8.03 us: spread_back(): jnp.einsum('rpgo,kigo->rpkgi', pre_split, kernel, preferred_element_type=...]
    ppermute x4 -> x0, starting transfers between devices: 14 us -> none  [the longest x2 6.31 us: from_behind(): return lax.ppermute(block, axis, route)]
    concatenate x2 -> x0, other arithmetic: 7.22 us -> none  [the longest x1 5.02 us: padded_2(): array = jnp.concatenate([before, array, after], axis=dim)]
  transfers between devices with their start and end apart: 5 -> 0, of which waited for: 1 -> 0; matrix products, arithmetic and copies ran while one was open for 4% -> 0% of each run, Pallas kernels for 0% -> 0%
where the time goes in v1:
time: 41.8 us; the launch traced here: 41.6 us
  Pallas kernels  34.3 us (82%)
  local copies, waits for them, and re-layouts  6.6 us (16%)
  between operations  0.64 us (2%)
    pallas_call x1, Pallas kernels, per_device(): pl.pallas_call(functools.partial(body, n_lat, n_lon, scale), out_shape=(j...  34.3 us
    unnamed x8, local copies, waits for them, and re-layouts  6.6 us

profile of v1, /device:TPU:0, one launch (start us, length us, event | category | flops | bytes accessed | tf_op | source)
XLA Modules:
  0.0 41.6 jit_solution(2306767261180981832)
XLA Ops:
  0.6 34.3 %conv_step.1 = (bf16[8,80,512]{2,1,0:T(8,128)(2,1)}, bf16[8,320,512]{2,1,0:T(8,128)(2,1)}, f32[16,128]{1,0:T(8,128)}, f32[16,128]{1,0:T(8,128)}) custom-call(bf16[8,320,512]{2,1,0:T(8,128)(2,1)} %x_hbm.1, bf16[512,512]{1,0:T(8,128)(2,1)} %wc_hbm.1, bf16[512,512]{1,0:T(8,128)(2,1)} %wp_hbm.1, bf16[8,80,512]{2,1,0:T(8,128)(2,1)} %cot_hbm.1), custom_call_target="tpu_custom_call" | custom-call | tf_op jit(solution)/shard_map/conv_step/pallas_call | solution.py:410
  35.0 2.0 %copy.14 = bf16[8,80,512]{2,1,0:T(8,128)(2,1)} copy(bf16[8,80,512]{2,1,0:T(8,128)(2,1)} %get-tuple-element.16) | data formatting | bytes 1310720
  36.9 0.0 copy-start.1
  36.9 0.0 copy-start
  36.9 3.4 %copy.15 = bf16[8,320,512]{2,1,0:T(8,128)(2,1)} copy(bf16[8,320,512]{2,1,0:T(8,128)(2,1)} %get-tuple-element.17) | data formatting | bytes 5242880
  40.4 0.0 copy-done.1
  40.4 0.6 %copy.16 = f32[512,4]{0,1:T(4,128)} copy(f32[512,4]{0,1:T(4,128)S(1)} %bitcast.11) | data formatting | bytes 16384
  41.0 0.0 copy-done
  41.0 0.6 %copy.17 = f32[512,4]{0,1:T(4,128)} copy(f32[512,4]{0,1:T(4,128)S(1)} %bitcast.10) | data formatting | bytes 16384
Async XLA Ops:
  36.9 3.4 %copy-start.1 = (f32[16,128]{1,0:T(8,128)S(1)}, f32[16,128]{1,0:T(8,128)}, u32[]{:S(2)}) copy-start(f32[16,128]{1,0:T(8,128)} %get-tuple-element.10) | copy-start | bytes 24580
  36.9 4.0 %copy-start = (f32[16,128]{1,0:T(8,128)S(1)}, f32[16,128]{1,0:T(8,128)}, u32[]{:S(2)}) copy-start(f32[16,128]{1,0:T(8,128)} %get-tuple-element.11) | copy-start | bytes 24580

commit v2 on v1

--- a/solution.py
+++ b/solution.py
@@ -36,42 +36,29 @@
     return jnp.concatenate(even, 0), jnp.concatenate(odd, 0)
 
 
-def body(
-    n_lat, n_lon, scale, x_hbm, wc_hbm, wp_hbm, cot_hbm,
-    enc_hbm, gin_hbm, gconv_ref, gpoint_ref,
-    xb, x32, wc, wp, cot, halo_w, halo_e, chalo_w, chalo_e, c32,
-    wd, pt, pe, preact, agrad, act, pre, pre_t, cot_t, pre32, pm, pp, enc, gout,
-    sums, csend, crecv, msend, mrecv,
-    x_sem, in_sem, out_sem, gout_sem, halo_send, halo_recv, c_sem_s, c_sem_r, m_sem_s, m_sem_r,
+def remote(src, dst, to, s, r):
+    return pltpu.make_async_remote_copy(
+        src_ref=src, dst_ref=dst, send_sem=s, recv_sem=r, device_id=to, device_id_type=MESH
+    )
+
+
+def open_body(
+    n_lon, x_hbm, wc_hbm, wp_hbm, cot_hbm, pt, wd, preact, agrad, cot_t,
+    xb, x32, wc, wp, cot, halo_w, halo_e, chalo_w, chalo_e, c32, pe,
+    x_sem, in_sem, halo_send, halo_recv,
 ):
     lat, cols = x_hbm.shape[0], x_hbm.shape[1]
     out_cols = cols // 4
     main = lat * out_cols
     span = cols + 16
-    pspan = out_cols + 16
     my_lat = lax.axis_index("lat")
     my_lon = lax.axis_index("lon")
-    core = lax.rem(my_lat, 2)
-    my_xhi = my_lat // 2
-    chips = (n_lat // 2) * n_lon
-    my_chip = my_xhi * n_lon + my_lon
-
-    def peer(i):
-        chip = lax.rem(my_chip + i, chips)
-        return (chip // n_lon * 2 + core, lax.rem(chip, n_lon))
-
-    partner = (my_xhi * 2 + 1 - core, my_lon)
     west = (my_lat, lax.rem(my_lon + n_lon - 1, n_lon))
     east = (my_lat, lax.rem(my_lon + 1, n_lon))
 
     barrier = pltpu.get_barrier_semaphore()
-
-    def say(i, carry):
-        pl.semaphore_signal(barrier, inc=1, device_id=peer(i), device_id_type=MESH)
-        return carry
-
-    lax.fori_loop(1, chips, say, 0)
-    pl.semaphore_signal(barrier, inc=1, device_id=partner, device_id_type=MESH)
+    for side in (west, east):
+        pl.semaphore_signal(barrier, inc=1, device_id=side, device_id_type=MESH)
 
     wc_copy = pltpu.make_async_copy(wc_hbm, wc, in_sem.at[0])
     wp_copy = pltpu.make_async_copy(wp_hbm, wp, in_sem.at[1])
@@ -81,10 +68,20 @@
         return pltpu.make_async_copy(x_hbm.at[r], xb.at[r], x_sem.at[r])
 
     wc_copy.start()
+    cot_copy.start()
+    wp_copy.start()
     for r in range(lat):
         x_copy(r).start()
-    cot_copy.start()
-    wp_copy.start()
+
+    pl.semaphore_wait(barrier, 2)
+    halos = [
+        remote(x_hbm.at[:, 0:8, :], halo_e, west, halo_send.at[0], halo_recv.at[0]),
+        remote(x_hbm.at[:, cols - 8 : cols, :], halo_w, east, halo_send.at[1], halo_recv.at[1]),
+        remote(cot_hbm.at[:, 0:8, :], chalo_e, west, halo_send.at[2], halo_recv.at[2]),
+        remote(cot_hbm.at[:, out_cols - 8 : out_cols, :], chalo_w, east, halo_send.at[3], halo_recv.at[3]),
+    ]
+    for h in halos:
+        h.start()
 
     wc_copy.wait()
     lane_group = lax.broadcasted_iota(jnp.int32, (64, HALF), 1) // 64
@@ -122,22 +119,6 @@
         return carry
 
     lax.fori_loop(0, lat, widen, 0)
-
-    pl.semaphore_wait(barrier, chips)
-
-    def remote(src, dst, to, s, r):
-        return pltpu.make_async_remote_copy(
-            src_ref=src, dst_ref=dst, send_sem=s, recv_sem=r, device_id=to, device_id_type=MESH
-        )
-
-    halos = [
-        remote(x_hbm.at[:, 0:8, :], halo_e, west, halo_send.at[0], halo_recv.at[0]),
-        remote(x_hbm.at[:, cols - 8 : cols, :], halo_w, east, halo_send.at[1], halo_recv.at[1]),
-        remote(cot_hbm.at[:, 0:8, :], chalo_e, west, halo_send.at[2], halo_recv.at[2]),
-        remote(cot_hbm.at[:, out_cols - 8 : out_cols, :], chalo_w, east, halo_send.at[3], halo_recv.at[3]),
-    ]
-    for h in halos:
-        h.start()
 
     cot_copy.wait()
     wp_copy.wait()
@@ -196,6 +177,39 @@
     ).astype(BF16)
     agrad[main : main + 16, :] = nt_dot(cot_edge, wp[...])
 
+
+def close_body(
+    n_lat, n_lon, scale, lat, cols, wp_hbm, pt, wd, preact, agrad, cot_t,
+    enc, gout, gconv_ref, gpoint_ref,
+    wp, act, pre, pre_t, pre32, pm, pp, g32, sums, csend, crecv, msend, mrecv,
+    in_sem, c_sem_s, c_sem_r, m_sem_s, m_sem_r,
+):
+    out_cols = cols // 4
+    main = lat * out_cols
+    pspan = out_cols + 16
+    my_lat = lax.axis_index("lat")
+    my_lon = lax.axis_index("lon")
+    core = lax.rem(my_lat, 2)
+    my_xhi = my_lat // 2
+    chips = (n_lat // 2) * n_lon
+    my_chip = my_xhi * n_lon + my_lon
+
+    def peer(i):
+        chip = lax.rem(my_chip + i, chips)
+        return (chip // n_lon * 2 + core, lax.rem(chip, n_lon))
+
+    partner = (my_xhi * 2 + 1 - core, my_lon)
+    barrier = pltpu.get_barrier_semaphore()
+
+    def say(i, carry):
+        pl.semaphore_signal(barrier, inc=1, device_id=peer(i), device_id_type=MESH)
+        return carry
+
+    lax.fori_loop(1, chips, say, 0, unroll=9)
+    pl.semaphore_signal(barrier, inc=1, device_id=partner, device_id_type=MESH)
+    wp_copy = pltpu.make_async_copy(wp_hbm, wp, in_sem.at[0])
+    wp_copy.start()
+
     def gelu(at, l):
         z = preact[l, at, :]
         z2 = z * z
@@ -233,8 +247,7 @@
             csend[which, 2 * i + 1] = odd.astype(BF16)
             return carry
 
-        lax.fori_loop(0, 32, one, 0)
-        pair(which).start()
+        lax.fori_loop(0, 32, one, 0, unroll=4)
 
     def pair(which):
         return remote(csend.at[which], crecv.at[which], partner, c_sem_s.at[which], c_sem_r.at[which])
@@ -248,7 +261,7 @@
             msend[which, 2 * i + 1] = (odd + crecv[which, 2 * i + 1].astype(F32)).astype(BF16)
             return carry
 
-        lax.fori_loop(0, 32, one, 0)
+        lax.fori_loop(0, 32, one, 0, unroll=4)
 
         def push(i, carry):
             chip = lax.rem(my_chip + i, chips)
@@ -257,7 +270,7 @@
             ).start()
             return carry
 
-        lax.fori_loop(1, chips, push, 0)
+        lax.fori_loop(1, chips, push, 0, unroll=9)
 
     def collect(which, out_ref):
         everything = pltpu.make_async_copy(
@@ -278,12 +291,7 @@
         rows = slice(c * HALF, (c + 1) * HALF)
         sums[0, rows, :] = dot(cot_t[rows, :], act[...])
     send_half(0)
-
-    enc[...] = dot(act[...], wp[...]).astype(BF16).reshape(lat, out_cols, C)
-    enc_copy = pltpu.make_async_copy(enc, enc_hbm, out_sem.at[0])
-    enc_copy.start()
     pre_t[...] = pre[...].T
-    send_all(0)
 
     low_lanes = lax.broadcasted_iota(jnp.int32, (64, 128), 1) < 64
 
@@ -307,6 +315,14 @@
 
     lax.fori_loop(0, KW // 2, conv_grad, 0)
     send_half(1)
+    pl.semaphore_wait(barrier, chips)
+    pair(0).start()
+    pair(1).start()
+
+    wp_copy.wait()
+    enc[...] = dot(act[...], wp[...]).astype(BF16).reshape(lat, out_cols, C)
+    send_all(0)
+    send_all(1)
 
     for r in range(lat):
         at = slice(r * out_cols, (r + 1) * out_cols)
@@ -314,14 +330,8 @@
             lanes = slice(l * 128, (l + 1) * 128)
             pm[at, lanes] = pre32[l, r * pspan + 7 : r * pspan + 7 + out_cols, :].astype(BF16)
             pp[at, lanes] = pre32[l, r * pspan + 9 : r * pspan + 9 + out_cols, :].astype(BF16)
-    send_all(1)
 
     gblock = 4
-
-    def gout_copy(c):
-        return pltpu.make_async_copy(
-            gout.at[pl.ds(c * gblock, gblock)], gin_hbm.at[pl.ds(c * gblock, gblock)], gout_sem.at[c]
-        )
 
     def input_grad(c, carry):
         rows = gblock * out_cols
@@ -335,26 +345,35 @@
                 )
                 for r in range(gblock):
                     for i in range(2):
-                        x32[2 * h + i, pl.ds((c * gblock + r) * cols + m, out_cols, stride=4), :] = y[
+                        g32[2 * h + i, pl.ds((c * gblock + r) * cols + m, out_cols, stride=4), :] = y[
                             r * out_cols : (r + 1) * out_cols, i * 128 : (i + 1) * 128
                         ]
         for r in range(gblock):
             row = c * gblock + r
             for s in range(0, cols, 16):
                 for l in range(4):
-                    gout[row, s : s + 16, l * 128 : (l + 1) * 128] = x32[
+                    gout[row, s : s + 16, l * 128 : (l + 1) * 128] = g32[
                         l, pl.ds(pl.multiple_of(row * cols + s, 16), 16), :
                     ].astype(BF16)
-        gout_copy(c).start()
         return carry
 
     lax.fori_loop(0, lat // gblock, input_grad, 0)
 
     collect(0, gpoint_ref)
     collect(1, gconv_ref)
-    enc_copy.wait()
-    for c in range(lat // gblock):
-        gout_copy(c).wait()
+
+
+def drain_body(enc, gout, conv, point, enc_hbm, gin_hbm, conv_hbm, point_hbm, sems):
+    moves = [
+        pltpu.make_async_copy(src, dst, sems.at[i])
+        for i, (src, dst) in enumerate(
+            ((gout, gin_hbm), (enc, enc_hbm), (conv, conv_hbm), (point, point_hbm))
+        )
+    ]
+    for m in moves:
+        m.start()
+    for m in moves:
+        m.wait()
 
 
 def per_device(n_lat, n_lon, inputs, w_conv, w_point, cotangent):
@@ -364,65 +383,93 @@
     chips = (n_lat // 2) * n_lon
     scale = 1.0 / math.sqrt(main * n_lat * n_lon)
     dma = pltpu.SemaphoreType.DMA
-    scratch = [
-        pltpu.VMEM((lat, cols, C), BF16),
-        pltpu.VMEM((4, lat * (cols + 16), 128), F32),
-        pltpu.VMEM((C, C), BF16),
-        pltpu.VMEM((C, C), BF16),
-        pltpu.VMEM((lat, out_cols, C), BF16),
-        pltpu.VMEM((lat, 8, C), BF16),
-        pltpu.VMEM((lat, 8, C), BF16),
-        pltpu.VMEM((lat, 8, C), BF16),
-        pltpu.VMEM((lat, 8, C), BF16),
-        pltpu.VMEM((4, 2 * lat * 8, 128), F32),
-        pltpu.VMEM((2, KW * HALF, HALF), BF16),
-        pltpu.VMEM((2, main, KW * HALF), BF16),
-        pltpu.VMEM((2, 32, KW * HALF), BF16),
-        pltpu.VMEM((4, main + 16, 128), F32),
-        pltpu.VMEM((main + 16, C), F32),
-        pltpu.VMEM((main, C), BF16),
-        pltpu.VMEM((main, C), BF16),
-        pltpu.VMEM((C, main), BF16),
-        pltpu.VMEM((C, main), BF16),
-        pltpu.VMEM((4, lat * (out_cols + 16), 128), F32),
-        pltpu.VMEM((main, C), BF16),
-        pltpu.VMEM((main, C), BF16),
-        pltpu.VMEM((lat, out_cols, C), BF16),
-        pltpu.VMEM((lat, cols, C), BF16),
-        pltpu.VMEM((2, C, C), F32),
-        pltpu.VMEM((2, chips, 16, 128), BF16),
-        pltpu.VMEM((2, chips, 16, 128), BF16),
-        pltpu.VMEM((2, chips, 16, 128), BF16),
-        pltpu.VMEM((2, chips - 1, 16, 128), BF16),
-        dma((lat,)),
-        dma((3,)),
-        dma((1,)),
-        dma((2,)),
-        dma((4,)),
-        dma((4,)),
-        dma((2,)),
-        dma((2,)),
-        dma((2,)),
-        dma((2,)),
-    ]
+    vmem = pltpu.VMEM
     any_spec = pl.BlockSpec(memory_space=pl.ANY)
     vmem_spec = pl.BlockSpec(memory_space=pltpu.VMEM)
+
+    handed = pl.pallas_call(
+        functools.partial(open_body, n_lon),
+        out_shape=(
+            vmem((2, main, KW * HALF), BF16),
+            vmem((2, KW * HALF, HALF), BF16),
+            vmem((4, main + 16, 128), F32),
+            vmem((main + 16, C), F32),
+            vmem((C, main), BF16),
+        ),
+        in_specs=[any_spec] * 4,
+        out_specs=(vmem_spec,) * 5,
+        scratch_shapes=[
+            vmem((lat, cols, C), BF16),
+            vmem((4, lat * (cols + 16), 128), F32),
+            vmem((C, C), BF16),
+            vmem((C, C), BF16),
+            vmem((lat, out_cols, C), BF16),
+            vmem((lat, 8, C), BF16),
+            vmem((lat, 8, C), BF16),
+            vmem((lat, 8, C), BF16),
+            vmem((lat, 8, C), BF16),
+            vmem((4, 2 * lat * 8, 128), F32),
+            vmem((2, 32, KW * HALF), BF16),
+            dma((lat,)),
+            dma((3,)),
+            dma((4,)),
+            dma((4,)),
+        ],
+        compiler_params=pltpu.CompilerParams(
+            collective_id=1, has_side_effects=True, vmem_limit_bytes=32 * 1024 * 1024
+        ),
+        name="forward_step",
+    )(inputs, w_conv, w_point, cotangent)
+
+    results = pl.pallas_call(
+        functools.partial(close_body, n_lat, n_lon, scale, lat, cols),
+        out_shape=(
+            vmem((lat, out_cols, C), BF16),
+            vmem((lat, cols, C), BF16),
+            vmem((16, 128), F32),
+            vmem((16, 128), F32),
+        ),
+        in_specs=[any_spec] + [vmem_spec] * 5,
+        out_specs=(vmem_spec,) * 4,
+        scratch_shapes=[
+            vmem((C, C), BF16),
+            vmem((main, C), BF16),
+            vmem((main, C), BF16),
+            vmem((C, main), BF16),
+            vmem((4, lat * (out_cols + 16), 128), F32),
+            vmem((main, C), BF16),
+            vmem((main, C), BF16),
+            vmem((4, lat * cols, 128), F32),
+            vmem((2, C, C), F32),
+            vmem((2, chips, 16, 128), BF16),
+            vmem((2, chips, 16, 128), BF16),
+            vmem((2, chips, 16, 128), BF16),
+            vmem((2, chips - 1, 16, 128), BF16),
+            dma((1,)),
+            dma((2,)),
+            dma((2,)),
+            dma((2,)),
+            dma((2,)),
+        ],
+        compiler_params=pltpu.CompilerParams(
+            collective_id=0, has_side_effects=True, vmem_limit_bytes=40 * 1024 * 1024
+        ),
+        name="backward_step",
+    )(w_point, *handed)
+
     encoded, grad_inputs, conv, point = pl.pallas_call(
-        functools.partial(body, n_lat, n_lon, scale),
+        drain_body,
         out_shape=(
             jax.ShapeDtypeStruct((lat, out_cols, C), BF16),
             jax.ShapeDtypeStruct((lat, cols, C), BF16),
             jax.ShapeDtypeStruct((16, 128), F32),
             jax.ShapeDtypeStruct((16, 128), F32),
         ),
-        in_specs=[any_spec] * 4,
-        out_specs=(any_spec, any_spec, vmem_spec, vmem_spec),
-        scratch_shapes=scratch,
-        compiler_params=pltpu.CompilerParams(
-            collective_id=0, has_side_effects=True, vmem_limit_bytes=60 * 1024 * 1024
-        ),
-        name="conv_step",
-    )(inputs, w_conv, w_point, cotangent)
+        in_specs=[vmem_spec] * 4,
+        out_specs=(any_spec,) * 4,
+        scratch_shapes=[dma((4,))],
+        name="drain",
+    )(*results)
 
     def unfold(block):
         return block.reshape(4, 4, 128).transpose(0, 2, 1).reshape(C, 4)

time: 41.8 us -> 45 us (1.077)
  local copies, waits for them, and re-layouts: 6.6 us -> 8.43 us
  Pallas kernels: 34.3 us -> 35.3 us
    unnamed x8 -> x18, local copies, waits for them, and re-layouts: 6.6 us -> 8.43 us
    pallas_call x1 -> x3, Pallas kernels: 34.3 us -> 35.3 us  [the longest x1 18.7 us: per_device(): pl.pallas_call(functools.partial(close_body, n_lat, n_lon, scale, lat, co...]
where the time goes in v2:
time: 45 us; the launch traced here: 44.4 us
  Pallas kernels  35.3 us (78%)
  local copies, waits for them, and re-layouts  8.43 us (19%)
  between operations  0.68 us (2%)
    pallas_call x1, Pallas kernels, per_device(): pl.pallas_call(functools.partial(close_body, n_lat, n_lon, scale, lat, co...  18.7 us
    pallas_call x1, Pallas kernels, per_device(): pl.pallas_call(functools.partial(open_body, n_lon), out_shape=(vmem((2, m...  13 us
    unnamed x18, local copies, waits for them, and re-layouts  8.43 us
    pallas_call x1, Pallas kernels, per_device(): pl.pallas_call(drain_body, out_shape=(jax.ShapeDtypeStruct((lat, out_cols...  3.61 us

profile of v2, /device:TPU:0, one launch (start us, length us, event | category | flops | bytes accessed | tf_op | source)
XLA Modules:
  0.0 44.4 jit_solution(11259275689611830403)
XLA Ops:
  0.6 0.0 copy-start
  0.6 1.7 %copy-done = bf16[8,320,512]{2,1,0:T(8,128)(2,1)S(1)} copy-done((bf16[8,320,512]{2,1,0:T(8,128)(2,1)S(1)}, bf16[8,320,512]{2,1,0:T(8,128)(2,1)}, u32[]{:S(2)}) %copy-start) | copy-done | bytes 2621464
  2.4 0.0 copy-start.2
  2.4 1.0 %copy-done.2 = bf16[512,512]{1,0:T(8,128)(2,1)S(1)} copy-done((bf16[512,512]{1,0:T(8,128)(2,1)S(1)}, bf16[512,512]{1,0:T(8,128)(2,1)}, u32[]{:S(2)}) %copy-start.2) | copy-done | bytes 524312
  3.4 0.0 copy-start.5
  3.4 1.1 %copy-done.5 = bf16[8,80,512]{2,1,0:T(8,128)(2,1)S(1)} copy-done((bf16[8,80,512]{2,1,0:T(8,128)(2,1)S(1)}, bf16[8,80,512]{2,1,0:T(8,128)(2,1)}, u32[]{:S(2)}) %copy-start.5) | copy-done | bytes 655384
  4.5 0.0 copy-start.6
  4.5 1.0 %copy-done.6 = bf16[512,512]{1,0:T(8,128)(2,1)S(1)} copy-done((bf16[512,512]{1,0:T(8,128)(2,1)S(1)}, bf16[512,512]{1,0:T(8,128)(2,1)}, u32[]{:S(2)}) %copy-start.6) | copy-done | bytes 524312
  5.5 0.0 copy-start.3
  5.5 13.0 %forward_step.1 = (bf16[2,640,2048]{2,1,0:T(8,128)(2,1)S(1)}, bf16[2,2048,256]{2,1,0:T(8,128)(2,1)S(1)}, f32[4,656,128]{2,1,0:T(8,128)S(1)}, f32[656,512]{1,0:T(8,128)S(1)}, bf16[512,640]{1,0:T(8,128)(2,1)S(1)}) custom-call(bf16[8,320,512]{2,1,0:T(8,128)(2,1)S(1)} %copy-done, bf16[512,512]{1,0:T(8,128)(2,1)S(1)} %copy-done.6, ...), custom_call_target="tpu_custom_call" | custom-call | tf_op jit(solution)/shard_map/forward_step/pallas_call | solution.py:390
  18.5 0.0 copy-done.3
  18.6 18.7 %backward_step.1 = (bf16[8,80,512]{2,1,0:T(8,128)(2,1)S(1)}, bf16[8,320,512]{2,1,0:T(8,128)(2,1)S(1)}, f32[16,128]{1,0:T(8,128)S(1)}, f32[16,128]{1,0:T(8,128)S(1)}) custom-call(bf16[512,512]{1,0:T(8,128)(2,1)S(1)} %copy-done.3, bf16[2,640,2048]{2,1,0:T(8,128)(2,1)S(1)} %get-tuple-element.17.pt, bf16[2,2048,256]{2,1,0:T(8,128)(2,1)S(1)} %get-tuple-element.18.wd, ...), custom_call_target="tpu_custom_call" | custom-call | tf_op jit(solution)/shard_map/backward_step/pallas_call | solution.py:424
  37.3 0.0 copy-start.1
  37.3 1.5 %copy-done.1 = bf16[8,320,512]{2,1,0:T(8,128)(2,1)} copy-done((bf16[8,320,512]{2,1,0:T(8,128)(2,1)}, bf16[8,320,512]{2,1,0:T(8,128)(2,1)S(1)}, u32[]{:S(2)}) %copy-start.1) | copy-done | bytes 2621464
  38.8 0.0 copy-start.4
  38.8 0.8 %copy-done.4 = bf16[8,80,512]{2,1,0:T(8,128)(2,1)} copy-done((bf16[8,80,512]{2,1,0:T(8,128)(2,1)}, bf16[8,80,512]{2,1,0:T(8,128)(2,1)S(1)}, u32[]{:S(2)}) %copy-start.4) | copy-done | bytes 655384
  39.6 0.0 copy-start.7
  39.6 0.6 %copy-done.7 = f32[16,128]{1,0:T(8,128)} copy-done((f32[16,128]{1,0:T(8,128)}, f32[16,128]{1,0:T(8,128)S(1)}, u32[]{:S(2)}) %copy-start.7) | copy-done | bytes 8216
  40.2 0.0 copy-start.8
  40.2 0.6 %copy-done.8 = f32[16,128]{1,0:T(8,128)} copy-done((f32[16,128]{1,0:T(8,128)}, f32[16,128]{1,0:T(8,128)S(1)}, u32[]{:S(2)}) %copy-start.8) | copy-done | bytes 8216
  40.8 3.6 %drain.1 = (bf16[8,80,512]{2,1,0:T(8,128)(2,1)}, bf16[8,320,512]{2,1,0:T(8,128)(2,1)}, f32[16,128]{1,0:T(8,128)}, f32[16,128]{1,0:T(8,128)}) custom-call(bf16[8,80,512]{2,1,0:T(8,128)(2,1)} %copy-done.4, bf16[8,320,512]{2,1,0:T(8,128)(2,1)} %copy-done.1, f32[16,128]{1,0:T(8,128)} %copy-done.7, f32[16,128]{1,0:T(8,128)} %copy-done.8), custom_call_target="tpu_custom_call" | custom-call | tf_op jit(solution)/shard_map/drain/pallas_call | solution.py:460
Async XLA Ops:
  0.6 1.7 %copy-start = (bf16[8,320,512]{2,1,0:T(8,128)(2,1)S(1)}, bf16[8,320,512]{2,1,0:T(8,128)(2,1)}, u32[]{:S(2)}) copy-start(bf16[8,320,512]{2,1,0:T(8,128)(2,1)} %x_hbm.1) | copy-start | bytes 7864324
  2.4 1.0 %copy-start.2 = (bf16[512,512]{1,0:T(8,128)(2,1)S(1)}, bf16[512,512]{1,0:T(8,128)(2,1)}, u32[]{:S(2)}) copy-start(bf16[512,512]{1,0:T(8,128)(2,1)} %wp_hbm.3) | copy-start | bytes 1572868
  3.4 1.1 %copy-start.5 = (bf16[8,80,512]{2,1,0:T(8,128)(2,1)S(1)}, bf16[8,80,512]{2,1,0:T(8,128)(2,1)}, u32[]{:S(2)}) copy-start(bf16[8,80,512]{2,1,0:T(8,128)(2,1)} %cot_hbm.1) | copy-start | bytes 1966084
  4.5 1.0 %copy-start.6 = (bf16[512,512]{1,0:T(8,128)(2,1)S(1)}, bf16[512,512]{1,0:T(8,128)(2,1)}, u32[]{:S(2)}) copy-start(bf16[512,512]{1,0:T(8,128)(2,1)} %wc_hbm.1) | copy-start | bytes 1572868
  5.5 13.0 %copy-start.3 = (bf16[512,512]{1,0:T(8,128)(2,1)S(1)}, bf16[512,512]{1,0:T(8,128)(2,1)}, u32[]{:S(2)}) copy-start(bf16[512,512]{1,0:T(8,128)(2,1)} %wp_hbm.3) | copy-start | bytes 1572868
  37.3 1.5 %copy-start.1 = (bf16[8,320,512]{2,1,0:T(8,128)(2,1)}, bf16[8,320,512]{2,1,0:T(8,128)(2,1)S(1)}, u32[]{:S(2)}) copy-start(bf16[8,320,512]{2,1,0:T(8,128)(2,1)S(1)} %get-tuple-element.23.gout) | copy-start | bytes 7864324
  38.8 0.8 %copy-start.4 = (bf16[8,80,512]{2,1,0:T(8,128)(2,1)}, bf16[8,80,512]{2,1,0:T(8,128)(2,1)S(1)}, u32[]{:S(2)}) copy-start(bf16[8,80,512]{2,1,0:T(8,128)(2,1)S(1)} %get-tuple-element.22.enc) | copy-start | bytes 1966084
  39.6 0.6 %copy-start.7 = (f32[16,128]{1,0:T(8,128)}, f32[16,128]{1,0:T(8,128)S(1)}, u32[]{:S(2)}) copy-start(f32[16,128]{1,0:T(8,128)S(1)} %get-tuple-element.24.conv) | copy-start | bytes 24580
  40.2 0.6 %copy-start.8 = (f32[16,128]{1,0:T(8,128)}, f32[16,128]{1,0:T(8,128)S(1)}, u32[]{:S(2)}) copy-start(f32[16,128]{1,0:T(8,128)S(1)} %get-tuple-element.25.point) | copy-start | bytes 24580

commit v3 on v2

--- a/solution.py
+++ b/solution.py
@@ -27,9 +27,8 @@
     return jnp.dot(a, b, preferred_element_type=F32)
 
 
-def messages(rows8):
+def messages(tiles):
     low = lax.broadcasted_iota(jnp.int32, (8, 128), 0) < 4
-    tiles = [rows8[:, l * 128 : (l + 1) * 128] for l in range(4)]
     rolled = [pltpu.roll(t, 4, 0) for t in tiles]
     even = [jnp.where(low, tiles[a], rolled[a + 1]) for a in (0, 2)]
     odd = [jnp.where(low, rolled[a], tiles[a + 1]) for a in (0, 2)]
@@ -43,8 +42,8 @@
 
 
 def open_body(
-    n_lon, x_hbm, wc_hbm, wp_hbm, cot_hbm, pt, wd, preact, agrad, cot_t,
-    xb, x32, wc, wp, cot, halo_w, halo_e, chalo_w, chalo_e, c32, pe,
+    n_lon, x_hbm, wc_hbm, cot_hbm, pt, wd, cot_edge,
+    xb, x32, wc, halo_w, halo_e, chalo_w, chalo_e, c32,
     x_sem, in_sem, halo_send, halo_recv,
 ):
     lat, cols = x_hbm.shape[0], x_hbm.shape[1]
@@ -61,15 +60,11 @@
         pl.semaphore_signal(barrier, inc=1, device_id=side, device_id_type=MESH)
 
     wc_copy = pltpu.make_async_copy(wc_hbm, wc, in_sem.at[0])
-    wp_copy = pltpu.make_async_copy(wp_hbm, wp, in_sem.at[1])
-    cot_copy = pltpu.make_async_copy(cot_hbm, cot, in_sem.at[2])
 
     def x_copy(r):
         return pltpu.make_async_copy(x_hbm.at[r], xb.at[r], x_sem.at[r])
 
     wc_copy.start()
-    cot_copy.start()
-    wp_copy.start()
     for r in range(lat):
         x_copy(r).start()
 
@@ -120,24 +115,6 @@
 
     lax.fori_loop(0, lat, widen, 0)
 
-    cot_copy.wait()
-    wp_copy.wait()
-    cot2 = cot[...].reshape(main, C)
-    cot_t[...] = cot2.T
-    agrad[0:main, :] = nt_dot(cot2, wp[...])
-
-    step = main // 2
-
-    def forward(c, carry):
-        at = pl.ds(pl.multiple_of(c * step, 16), step)
-        for h in range(2):
-            y = dot(pt[h, at, :], wd[h])
-            for i in range(2):
-                preact[2 * h + i, at, :] = y[:, i * 128 : (i + 1) * 128]
-        return carry
-
-    lax.fori_loop(0, 2, forward, 0)
-
     for h in halos:
         h.wait()
     for r in range(lat):
@@ -154,34 +131,17 @@
                 pt[l // 2, r * out_cols + j : r * out_cols + j + 16, tap_lanes(k, l)] = taken
     for k in range(KW):
         for l in range(4):
-            rows = [
-                x32[l, pl.ds(4 * j + 6 + k, lat, stride=span), :]
-                for j in (-1, out_cols, 0, out_cols - 1)
-            ]
-            pe[l // 2, :, tap_lanes(k, l)] = jnp.concatenate(rows, 0).astype(BF16)
-    for h in range(2):
-        edge = dot(pe[h], wd[h])
-        for i in range(2):
-            part = edge[:, i * 128 : (i + 1) * 128]
-            preact[2 * h + i, main : main + 16, :] = part[0:16]
-            preact[2 * h + i, pl.ds(0, lat, stride=out_cols), :] = part[16:24]
-            preact[2 * h + i, pl.ds(out_cols - 1, lat, stride=out_cols), :] = part[24:32]
-    cot_edge = jnp.concatenate(
-        [
-            jnp.concatenate(
-                [c32[l, pl.ds(7, lat, stride=8), :], c32[l, pl.ds(lat * 8, lat, stride=8), :]], 0
-            )
-            for l in range(4)
-        ],
-        1,
-    ).astype(BF16)
-    agrad[main : main + 16, :] = nt_dot(cot_edge, wp[...])
+            rows = [x32[l, pl.ds(4 * j + 6 + k, lat, stride=span), :] for j in (-1, out_cols)]
+            pt[l // 2, main : main + 16, tap_lanes(k, l)] = jnp.concatenate(rows, 0).astype(BF16)
+    for l in range(4):
+        rows = [c32[l, pl.ds(7, lat, stride=8), :], c32[l, pl.ds(lat * 8, lat, stride=8), :]]
+        cot_edge[:, l * 128 : (l + 1) * 128] = jnp.concatenate(rows, 0).astype(BF16)
 
 
 def close_body(
-    n_lat, n_lon, scale, lat, cols, wp_hbm, pt, wd, preact, agrad, cot_t,
+    n_lat, n_lon, scale, lat, cols, wp_hbm, cot_hbm, pt, wd, cot_edge,
     enc, gout, gconv_ref, gpoint_ref,
-    wp, act, pre, pre_t, pre32, pm, pp, g32, sums, csend, crecv, msend, mrecv,
+    wp, cot, preact, agrad, cot_t, act, pre, pre_t, pre32, pm, pp, g32, sums, crecv, msend, mrecv,
     in_sem, c_sem_s, c_sem_r, m_sem_s, m_sem_r,
 ):
     out_cols = cols // 4
@@ -208,7 +168,30 @@
     lax.fori_loop(1, chips, say, 0, unroll=9)
     pl.semaphore_signal(barrier, inc=1, device_id=partner, device_id_type=MESH)
     wp_copy = pltpu.make_async_copy(wp_hbm, wp, in_sem.at[0])
+    cot_copy = pltpu.make_async_copy(cot_hbm, cot, in_sem.at[1])
     wp_copy.start()
+    cot_copy.start()
+
+    def forward(rows):
+        for h in range(2):
+            y = dot(pt[h, rows, :], wd[h])
+            for i in range(2):
+                preact[2 * h + i, rows, :] = y[:, i * 128 : (i + 1) * 128]
+
+    step = main // 2
+
+    def forward_part(c, carry):
+        forward(pl.ds(pl.multiple_of(c * step, 16), step))
+        return carry
+
+    lax.fori_loop(0, 2, forward_part, 0)
+    forward(slice(main, main + 16))
+    wp_copy.wait()
+    cot_copy.wait()
+    cot2 = cot[...].reshape(main, C)
+    cot_t[...] = cot2.T
+    agrad[0:main, :] = nt_dot(cot2, wp[...])
+    agrad[main : main + 16, :] = nt_dot(cot_edge[...], wp[...])
 
     def gelu(at, l):
         z = preact[l, at, :]
@@ -237,28 +220,21 @@
         pre32[l, pl.ds(7, lat, stride=pspan), :] = edge_pre[0:8]
         pre32[l, pl.ds(8 + out_cols, lat, stride=pspan), :] = edge_pre[8:16]
 
-    def core_rows(q, i):
-        return pl.ds(pl.multiple_of((i // 16) * HALF + q * 128 + lax.rem(i, 16) * 8, 8), 8)
-
-    def send_half(which):
+    def pair(which, p):
+        return remote(
+            sums.at[which, p, :, 1 - core], crecv.at[which, p], partner, c_sem_s.at[which, p], c_sem_r.at[which, p]
+        )
+
+    def send_all(which):
+        for p in range(4):
+            pair(which, p).wait()
+
         def one(i, carry):
-            even, odd = messages(sums[which, core_rows(1 - core, i), :])
-            csend[which, 2 * i] = even.astype(BF16)
-            csend[which, 2 * i + 1] = odd.astype(BF16)
-            return carry
-
-        lax.fori_loop(0, 32, one, 0, unroll=4)
-
-    def pair(which):
-        return remote(csend.at[which], crecv.at[which], partner, c_sem_s.at[which], c_sem_r.at[which])
-
-    def send_all(which):
-        pair(which).wait()
-
-        def one(i, carry):
-            even, odd = messages(sums[which, core_rows(core, i), :])
-            msend[which, 2 * i] = (even + crecv[which, 2 * i].astype(F32)).astype(BF16)
-            msend[which, 2 * i + 1] = (odd + crecv[which, 2 * i + 1].astype(F32)).astype(BF16)
+            at = pl.ds(pl.multiple_of(lax.rem(i, 16) * 8, 8), 8)
+            x_hi = i // 16
+            even, odd = messages([sums[which, l, x_hi, core, at, :] + crecv[which, l, x_hi, at, :] for l in range(4)])
+            msend[which, 2 * i] = even.astype(BF16)
+            msend[which, 2 * i + 1] = odd.astype(BF16)
             return carry
 
         lax.fori_loop(0, 32, one, 0, unroll=4)
@@ -287,11 +263,15 @@
         total = lax.fori_loop(0, chips - 1, one, msend[which, my_chip].astype(F32), unroll=7)
         out_ref[...] = total * scale
 
-    for c in range(2):
-        rows = slice(c * HALF, (c + 1) * HALF)
-        sums[0, rows, :] = dot(cot_t[rows, :], act[...])
-    send_half(0)
+    for x_hi in range(2):
+        y = dot(cot_t[x_hi * HALF : (x_hi + 1) * HALF, :], act[...])
+        for l in range(4):
+            for q in range(2):
+                sums[0, l, x_hi, q] = y[q * 128 : (q + 1) * 128, l * 128 : (l + 1) * 128]
     pre_t[...] = pre[...].T
+    pl.semaphore_wait(barrier, chips)
+    for p in range(4):
+        pair(0, p).start()
 
     low_lanes = lax.broadcasted_iota(jnp.int32, (64, 128), 1) < 64
 
@@ -308,21 +288,15 @@
                     b = pltpu.roll(b, 64, 1)
                 else:
                     a = pltpu.roll(a, 64, 1)
-                sums[1, h * HALF + g * 64 : h * HALF + g * 64 + 64, pl.ds(pl.multiple_of(p * 128, 128), 128)] = (
-                    jnp.where(low_lanes, a, b)
-                )
+                half = (g % 2) * 64
+                sums[1, p, h, g // 2, half : half + 64, :] = jnp.where(low_lanes, a, b)
+        pair(1, p).start()
         return carry
 
     lax.fori_loop(0, KW // 2, conv_grad, 0)
-    send_half(1)
-    pl.semaphore_wait(barrier, chips)
-    pair(0).start()
-    pair(1).start()
-
-    wp_copy.wait()
-    enc[...] = dot(act[...], wp[...]).astype(BF16).reshape(lat, out_cols, C)
     send_all(0)
     send_all(1)
+    enc[...] = dot(act[...], wp[...]).astype(BF16).reshape(lat, out_cols, C)
 
     for r in range(lat):
         at = slice(r * out_cols, (r + 1) * out_cols)
@@ -384,42 +358,40 @@
     scale = 1.0 / math.sqrt(main * n_lat * n_lon)
     dma = pltpu.SemaphoreType.DMA
     vmem = pltpu.VMEM
-    any_spec = pl.BlockSpec(memory_space=pl.ANY)
+    any_spec = pl.BlockSpec(memory_space=pltpu.HBM)
     vmem_spec = pl.BlockSpec(memory_space=pltpu.VMEM)
 
+    inputs, w_conv, w_point, cotangent = (
+        pltpu.with_memory_space_constraint(a, pltpu.HBM) for a in (inputs, w_conv, w_point, cotangent)
+    )
     handed = pl.pallas_call(
         functools.partial(open_body, n_lon),
         out_shape=(
-            vmem((2, main, KW * HALF), BF16),
+            vmem((2, main + 16, KW * HALF), BF16),
             vmem((2, KW * HALF, HALF), BF16),
-            vmem((4, main + 16, 128), F32),
-            vmem((main + 16, C), F32),
-            vmem((C, main), BF16),
-        ),
-        in_specs=[any_spec] * 4,
-        out_specs=(vmem_spec,) * 5,
+            vmem((16, C), BF16),
+        ),
+        in_specs=[any_spec] * 3,
+        out_specs=(vmem_spec,) * 3,
         scratch_shapes=[
             vmem((lat, cols, C), BF16),
             vmem((4, lat * (cols + 16), 128), F32),
             vmem((C, C), BF16),
-            vmem((C, C), BF16),
-            vmem((lat, out_cols, C), BF16),
             vmem((lat, 8, C), BF16),
             vmem((lat, 8, C), BF16),
             vmem((lat, 8, C), BF16),
             vmem((lat, 8, C), BF16),
             vmem((4, 2 * lat * 8, 128), F32),
-            vmem((2, 32, KW * HALF), BF16),
             dma((lat,)),
-            dma((3,)),
+            dma((1,)),
             dma((4,)),
             dma((4,)),
         ],
         compiler_params=pltpu.CompilerParams(
             collective_id=1, has_side_effects=True, vmem_limit_bytes=32 * 1024 * 1024
         ),
-        name="forward_step",
-    )(inputs, w_conv, w_point, cotangent)
+        name="halo_step",
+    )(inputs, w_conv, cotangent)
 
     results = pl.pallas_call(
         functools.partial(close_body, n_lat, n_lon, scale, lat, cols),
@@ -429,10 +401,14 @@
             vmem((16, 128), F32),
             vmem((16, 128), F32),
         ),
-        in_specs=[any_spec] + [vmem_spec] * 5,
+        in_specs=[any_spec] * 2 + [vmem_spec] * 3,
         out_specs=(vmem_spec,) * 4,
         scratch_shapes=[
             vmem((C, C), BF16),
+            vmem((lat, out_cols, C), BF16),
+            vmem((4, main + 16, 128), F32),
+            vmem((main + 16, C), F32),
+            vmem((C, main), BF16),
             vmem((main, C), BF16),
             vmem((main, C), BF16),
             vmem((C, main), BF16),
@@ -440,22 +416,21 @@
             vmem((main, C), BF16),
             vmem((main, C), BF16),
             vmem((4, lat * cols, 128), F32),
-            vmem((2, C, C), F32),
-            vmem((2, chips, 16, 128), BF16),
-            vmem((2, chips, 16, 128), BF16),
+            vmem((2, 4, 2, 2, 128, 128), F32),
+            vmem((2, 4, 2, 128, 128), F32),
             vmem((2, chips, 16, 128), BF16),
             vmem((2, chips - 1, 16, 128), BF16),
-            dma((1,)),
             dma((2,)),
-            dma((2,)),
+            dma((2, 4)),
+            dma((2, 4)),
             dma((2,)),
             dma((2,)),
         ],
         compiler_params=pltpu.CompilerParams(
             collective_id=0, has_side_effects=True, vmem_limit_bytes=40 * 1024 * 1024
         ),
-        name="backward_step",
-    )(w_point, *handed)
+        name="layer_step",
+    )(w_point, cotangent, *handed)
 
     encoded, grad_inputs, conv, point = pl.pallas_call(
         drain_body,
@@ -468,6 +443,7 @@
         in_specs=[vmem_spec] * 4,
         out_specs=(any_spec,) * 4,
         scratch_shapes=[dma((4,))],
+        compiler_params=pltpu.CompilerParams(vmem_limit_bytes=8 * 1024 * 1024),
         name="drain",
     )(*results)
 

time: 45 us -> 34.2 us (0.76); the launches traced: 44.4 us -> 34.1 us
  local copies, waits for them, and re-layouts: 8.43 us -> 0 us
  Pallas kernels: 35.3 us -> 33.5 us
    unnamed x18 -> x0, local copies, waits for them, and re-layouts: 8.43 us -> none
    pallas_call x1, Pallas kernels: 3.61 us -> 1.74 us  [per_device(): pl.pallas_call(drain_body, out_shape=(jax.ShapeDtypeStruct((lat, out_cols...]
    pallas_call x1, Pallas kernels: 18.7 us -> 19.9 us  [per_device(): pl.pallas_call(functools.partial(close_body, n_lat, n_lon, scale, lat, co...]
    pallas_call x1, Pallas kernels: 13 us -> 11.8 us  [per_device(): pl.pallas_call(functools.partial(open_body, n_lon), out_shape=(vmem((2, m...]
where the time goes in v3:
time: 34.2 us; the launch traced here: 34.1 us
  Pallas kernels  33.5 us (98%)
  between operations  0.65 us (2%)
    pallas_call x1, Pallas kernels, per_device(): pl.pallas_call(functools.partial(close_body, n_lat, n_lon, scale, lat, co...  19.9 us
    pallas_call x1, Pallas kernels, per_device(): pl.pallas_call(functools.partial(open_body, n_lon), out_shape=(vmem((2, m...  11.8 us
    pallas_call x1, Pallas kernels, per_device(): pl.pallas_call(drain_body, out_shape=(jax.ShapeDtypeStruct((lat, out_cols...  1.74 us

profile of v3, /device:TPU:0, one launch (start us, length us, event | category | flops | bytes accessed | tf_op | source)
XLA Modules:
  0.0 34.1 jit_solution(2515783413837959407)
XLA Ops:
  0.6 11.8 %halo_step.1 = (bf16[2,656,2048]{2,1,0:T(8,128)(2,1)S(1)}, bf16[2,2048,256]{2,1,0:T(8,128)(2,1)S(1)}, bf16[16,512]{1,0:T(8,128)(2,1)S(1)}) custom-call(bf16[8,320,512]{2,1,0:T(8,128)(2,1)} %x_hbm.1, bf16[512,512]{1,0:T(8,128)(2,1)} %wc_hbm.1, bf16[8,80,512]{2,1,0:T(8,128)(2,1)} %cot_hbm.3), custom_call_target="tpu_custom_call" | custom-call | tf_op jit(solution)/shard_map/halo_step/pallas_call | solution.py:367
  12.4 19.9 %layer_step.1 = (bf16[8,80,512]{2,1,0:T(8,128)(2,1)S(1)}, bf16[8,320,512]{2,1,0:T(8,128)(2,1)S(1)}, f32[16,128]{1,0:T(8,128)S(1)}, f32[16,128]{1,0:T(8,128)S(1)}) custom-call(bf16[512,512]{1,0:T(8,128)(2,1)} %wp_hbm.1, bf16[8,80,512]{2,1,0:T(8,128)(2,1)} %cot_hbm.3, bf16[2,656,2048]{2,1,0:T(8,128)(2,1)S(1)} %get-tuple-element.15.pt, ...), custom_call_target="tpu_custom_call" | custom-call | tf_op jit(solution)/shard_map/layer_step/pallas_call | solution.py:396
  32.4 1.7 %drain.1 = (bf16[8,80,512]{2,1,0:T(8,128)(2,1)}, bf16[8,320,512]{2,1,0:T(8,128)(2,1)}, f32[16,128]{1,0:T(8,128)}, f32[16,128]{1,0:T(8,128)}) custom-call(bf16[8,80,512]{2,1,0:T(8,128)(2,1)S(1)} %get-tuple-element.18.enc, bf16[8,320,512]{2,1,0:T(8,128)(2,1)S(1)} %get-tuple-element.19.gout, f32[16,128]{1,0:T(8,128)S(1)} %get-tuple-element.20.conv, ...), custom_call_target="tpu_custom_call" | custom-call | tf_op jit(solution)/shard_map/drain/pallas_call | solution.py:435
